TPU v7x, 32 devices: a whole 2x2x4 slice. The times are simulated.
32 devices in a mesh: clip: 2 (over y), tm: 4 (over z), head: 2 (over x), sub: 2 (over core).
Axes of the slice: x: 2, y: 2, z: 4, core: 2. Of those that a mesh axis runs over, the one named last changes fastest.
Arguments:
- queries: bfloat16 [8, 256, 3072], P(('clip', 'tm'), None, ('head', 'sub')), parts along dimension 0, may hold values from -6 to 6, as said below
- keys: bfloat16 [8, 256, 3072], P(('clip', 'tm'), None, ('head', 'sub')), parts along dimension 0, may hold values from -6 to 6, as said below
- values: bfloat16 [8, 256, 3072], P(('clip', 'tm'), None, ('head', 'sub')), parts along dimension 0, may hold values from -6 to 6
- band_table: int32 [4, 4], replicated, may hold values from 0 to 3, as said below
- windows: int32 [7], replicated, may hold values from 1 to 128, as said below
- out_weight: bfloat16 [3072, 3072], P(('head', 'sub')), may hold values from -0.109375 to 0.109375
Outputs:
- mixed: bfloat16 [8, 256, 3072], P(('clip', 'tm'), ('head', 'sub')), parts along dimension 0
There are 2 independent parts, one for each index of `clip`. A program takes and returns all parts, laid end to end along the dimension named above; an argument that names none is the same for every part. Nothing has to cross between parts.
Inputs may be any that keep to these rules, and one draw needn't show every extreme that they name: `queries`: entries of normal law within the range; some rows may be aligned with some key rows. `keys`: entries of normal law within the range; some rows may be aligned with some query rows. `band_table`: Symmetric; 0 exactly on the diagonal; off the diagonal, for frames at distance d it is floor(log2 d) + 1 or one more, never above 6; the pair of frames 0 and 3 takes the one more (up to 6). windows[0] = 128; for k >= 1, windows[k] lies between max(1, 64 // 2**k) and max(that + 1, 128 // 2**k + 1) - 1.
All inputs are finite; a program needn't handle non-finite values.
Results may differ from a plain program's by a relative error of at most 0.015.
Values may be sent and summed in bfloat16 or wider, within the bound.
A program may use at most 64 MiB of HBM per device.

v0:
```python
import functools

import jax
import jax.numpy as jnp
from jax import lax
from jax.experimental import pallas as pl
from jax.experimental.pallas import tpu as pltpu
from jax.sharding import PartitionSpec as P

HEAD = 128
MESH = pl.DeviceIdType.MESH


def local(queries, keys, values, band_table, windows, out_weight):
    frames, length, width = queries.shape
    heads = width // HEAD
    scale = HEAD ** (-0.5)
    here = lax.axis_index("tm") * frames
    query = queries[0].reshape(length, heads, HEAD)
    places = lax.iota(jnp.int32, length)
    gap = jnp.abs(places[:, None] - places[None, :])

    def absorb(carry, key_frame, value_frame, frame, usable):
        peak, total, numer = carry
        reach = windows[band_table[here, frame]]
        allowed = (gap <= reach)[None] & usable
        scores = (
            jnp.einsum(
                "phd,qhd->hpq",
                query,
                key_frame.reshape(length, heads, HEAD),
                preferred_element_type=jnp.float32,
            )
            * scale
        )
        masked = jnp.where(allowed, scores, jnp.float32(-1e30))
        top = jnp.maximum(peak, jnp.max(masked, axis=-1))
        weights = jnp.where(allowed, jnp.exp(scores - top[:, :, None]), jnp.float32(0.0))
        shrink = jnp.exp(peak - top)
        total = total * shrink + jnp.sum(weights, axis=-1)
        added = jnp.einsum(
            "hpq,qhd->phd",
            weights.astype(jnp.bfloat16),
            value_frame.reshape(length, heads, HEAD),
            preferred_element_type=jnp.float32,
        )
        numer = numer * jnp.transpose(shrink)[:, :, None] + added
        return (top, total, numer)

    carry = (
        jnp.full((heads, length), -1e30, jnp.float32),
        jnp.zeros((heads, length), jnp.float32),
        jnp.zeros((length, heads, HEAD), jnp.float32),
    )
    skipped = -1
    state = carry
    key_part = lax.all_gather(keys, "tm", axis=0, tiled=True)
    value_part = lax.all_gather(values, "tm", axis=0, tiled=True)

    def advance(inner, item):
        key_frame, value_frame, offset = item
        usable = jnp.abs(offset - here) > skipped
        return (absorb(inner, key_frame, value_frame, offset, usable), None)

    state, unused = lax.scan(
        advance, state, (key_part, value_part, lax.iota(jnp.int32, key_part.shape[0]))
    )
    carry = state
    peak, total, numer = carry
    attended = (
        (numer / jnp.transpose(total)[:, :, None]).astype(jnp.bfloat16).reshape(length, width)
    )
    mixed = lax.psum_scatter(
        jnp.dot(attended, out_weight, preferred_element_type=jnp.float32).astype(jnp.bfloat16),
        ("head", "sub"),
        scatter_dimension=0,
        tiled=True,
    )
    return mixed[None]


def fused_kernel(
    n, pieces, chunks, q_hbm, k_hbm, v_hbm, band_hbm, windows_hbm, w_hbm, out_ref,
    band, windows, asked, buf, weight, done, att, send_a, recv_a, send_b, recv_b, acc, own,
    in_send, in_recv, back_send, back_recv, a_send, a_recv, b_send, b_recv, w_sem, table_sem,
):
    frame = lax.axis_index("tm")
    row = lax.axis_index("head")
    core = lax.axis_index("sub")
    length = k_hbm.shape[1]
    block = length // 4
    slab = block // pieces
    heads = 2 * n - 2
    owner = [(h + 1) // 2 for h in range(heads)]
    slot = [1 if h > 0 and h % 2 == 0 else 0 for h in range(heads)]
    scale = HEAD ** (-0.5)

    barrier = pltpu.get_barrier_semaphore()
    for step in range(1, n):
        pl.semaphore_signal(
            barrier, inc=1, device_id={"tm": lax.rem(frame + step, n)}, device_id_type=MESH
        )
    pl.semaphore_signal(barrier, inc=1, device_id={"head": 1 - row}, device_id_type=MESH)
    pl.semaphore_signal(barrier, inc=1, device_id={"sub": 1 - core}, device_id_type=MESH)
    pl.semaphore_wait(barrier, n + 1)

    low = frame < n // 2

    def ends(h, a):
        columns = slice(h * HEAD, (h + 1) * HEAD)
        if a < 2:
            return (k_hbm, v_hbm)[a].at[0, :, columns], buf.at[slot[h], a, frame]
        p = a - 2
        source = q_hbm.at[:, p * slab : (p + 1) * slab, columns]
        return source, asked.at[slot[h], p, frame]

    def outgoing(h, a):
        source, target = ends(h, a)
        return pltpu.make_async_remote_copy(
            src_ref=source,
            dst_ref=target,
            send_sem=in_send.at[h, a],
            recv_sem=in_recv.at[slot[h], a, frame],
            device_id={"tm": owner[h]},
            device_id_type=MESH,
        )

    def send_head(h, ready, which):
        @pl.when(jnp.logical_and(ready, frame != owner[h]))
        def _():
            for a in which:
                outgoing(h, a).start()

    def send_slot(s, which):
        below = [h for h in range(heads) if slot[h] == s and owner[h] < n // 2]
        above = [h for h in reversed(range(heads)) if slot[h] == s and owner[h] >= n // 2]
        for h in above:
            send_head(h, low, which)
        for h in below:
            send_head(h, frame >= 0, which)
        for h in above:
            send_head(h, jnp.logical_not(low), which)

    send_slot(1, (0, 2))
    send_slot(0, (0, 2))
    send_slot(1, (1,))
    send_slot(0, (1,))
    for p in range(1, pieces):
        send_slot(1, (2 + p,))
        send_slot(0, (2 + p,))
    for h in range(heads):

        @pl.when(frame == owner[h])
        def _():
            for a in range(2 + pieces):
                source, target = ends(h, a)
                pltpu.make_async_copy(source, target, in_recv.at[slot[h], a, frame]).start()

    load_weight = pltpu.make_async_copy(w_hbm, weight, w_sem)
    load_weight.start()
    tables = (
        pltpu.make_async_copy(band_hbm, band, table_sem.at[0]),
        pltpu.make_async_copy(windows_hbm, windows, table_sem.at[1]),
    )
    for table in tables:
        table.start()

    for table in tables:
        table.wait()
    height = 4 * slab
    spot = lax.broadcasted_iota(jnp.int32, (height, length), 0)
    spot = (spot // slab) * block + lax.rem(spot, slab)
    spot = spot - lax.broadcasted_iota(jnp.int32, (height, length), 1)

    def returning(s, h, p, i):
        return pltpu.make_async_remote_copy(
            src_ref=done.at[s, p, i],
            dst_ref=att.at[p, :, pl.ds(pl.multiple_of(h * HEAD, HEAD), HEAD)],
            send_sem=back_send.at[s, p, i],
            recv_sem=back_recv.at[p, h],
            device_id={"tm": i},
            device_id_type=MESH,
        )

    def arrive(s, p):
        for j in range(n):
            for a in (0, 1) if p == 0 else ():
                pltpu.make_async_copy(buf.at[s, a, j], buf.at[s, a, j], in_recv.at[s, a, j]).wait()
            here = asked.at[s, p, j]
            pltpu.make_async_copy(here, here, in_recv.at[s, 2 + p, j]).wait()

    def attend(s, h, p):
        gap = jnp.abs(spot + p * slab)

        def one(step, carry):
            i = lax.rem(frame + 1 + step, n)
            query = asked[s, p, i].reshape(height, HEAD)
            parts = []
            top = None
            for j in range(n):
                score = lax.dot_general(
                    query, buf[s, 0, j], (((1,), (1,)), ((), ())),
                    preferred_element_type=jnp.float32,
                ) * scale
                score = jnp.where(gap <= windows[band[i, j]], score, jnp.float32(-1e30))
                peak = jnp.max(score, axis=-1, keepdims=True)
                top = peak if top is None else jnp.maximum(top, peak)
                parts.append(score)
            total = None
            numer = None
            for j in range(n):
                part = jnp.exp(parts[j] - top)
                added = jnp.sum(part, axis=-1, keepdims=True)
                product = jnp.dot(
                    part.astype(jnp.bfloat16), buf[s, 1, j], preferred_element_type=jnp.float32
                )
                total = added if total is None else total + added
                numer = product if numer is None else numer + product
            result = (numer / total).astype(jnp.bfloat16)

            @pl.when(i != frame)
            def _():
                done[s, p, i] = result
                returning(s, h, p, i).start()

            @pl.when(i == frame)
            def _():
                att[p, :, pl.ds(pl.multiple_of(h * HEAD, HEAD), HEAD)] = result

            return carry

        lax.fori_loop(0, n, one, 0)

    first = 2 * frame - (frame + n - 1) // n
    second = 2 * frame
    both = jnp.logical_and(frame > 0, frame < n - 1)
    for p in range(pieces):
        @pl.when(both)
        def _():
            arrive(1, p)
            attend(1, second, p)

        arrive(0, p)
        attend(0, first, p)

    load_weight.wait()
    width = weight.shape[1] // chunks

    def rows(p, who):
        return jnp.concatenate(
            [
                att[p, pl.ds(pl.multiple_of((r * 2 + who) * slab, slab), slab), :]
                for r in (row, 1 - row)
            ],
            axis=0,
        )

    def give_a(p, c):
        return pltpu.make_async_remote_copy(
            src_ref=send_a.at[p, c], dst_ref=recv_a.at[p, c],
            send_sem=a_send.at[p, c], recv_sem=a_recv.at[p, c],
            device_id={"sub": 1 - core}, device_id_type=MESH,
        )

    def give_b(p, c):
        return pltpu.make_async_remote_copy(
            src_ref=send_b.at[p, c], dst_ref=recv_b.at[p, c],
            send_sem=b_send.at[p, c], recv_sem=b_recv.at[p, c],
            device_id={"head": 1 - row}, device_id_type=MESH,
        )

    for p in range(pieces):
        for h in range(heads):

            @pl.when(frame != owner[h])
            def _():
                here = att.at[p, :, h * HEAD : (h + 1) * HEAD]
                pltpu.make_async_copy(here, here, back_recv.at[p, h]).wait()

        tokens = jnp.concatenate([rows(p, 1 - core), rows(p, core)], axis=0)
        for c in range(chunks):
            share = jnp.dot(
                tokens, weight[:, c * width : (c + 1) * width], preferred_element_type=jnp.float32
            )
            send_a[p, c] = share[: 2 * slab].astype(jnp.bfloat16)
            give_a(p, c).start()
            own[c] = share[2 * slab :]
        for c in range(chunks):
            give_a(p, c).wait_recv()
            both_cores = own[c] + recv_a[p, c].astype(jnp.float32)
            send_b[p, c] = both_cores[slab:].astype(jnp.bfloat16)
            give_b(p, c).start()
            acc[p, c] = both_cores[:slab]

    for p in range(pieces):
        for c in range(chunks):
            give_b(p, c).wait_recv()
            out_ref[p * slab : (p + 1) * slab, c * width : (c + 1) * width] = (
                acc[p, c] + recv_b[p, c].astype(jnp.float32)
            ).astype(jnp.bfloat16)

    for p in range(pieces):
        for c in range(chunks):
            give_a(p, c).wait_send()
            give_b(p, c).wait_send()
    for h in range(heads):

        @pl.when(frame != owner[h])
        def _():
            for a in range(2 + pieces):
                outgoing(h, a).wait_send()

    for i in range(n):

        @pl.when(i != frame)
        def _():
            for p in range(pieces):
                returning(0, first, p, i).wait_send()

        @pl.when(jnp.logical_and(both, i != frame))
        def _():
            for p in range(pieces):
                returning(1, second, p, i).wait_send()


def fused(n, queries, keys, values, band_table, windows, out_weight):
    length, width = queries.shape[1:]
    columns = out_weight.shape[1]
    heads = width // HEAD
    block = length // 4
    chunks = 2
    pieces = 2
    slab = block // pieces
    part = columns // chunks
    anywhere = pl.BlockSpec(memory_space=pl.ANY)
    dma = pltpu.SemaphoreType.DMA
    mixed = pl.pallas_call(
        functools.partial(fused_kernel, n, pieces, chunks),
        out_shape=jax.ShapeDtypeStruct((block, columns), jnp.bfloat16),
        in_specs=[anywhere] * 6,
        out_specs=pl.BlockSpec(memory_space=pltpu.VMEM),
        scratch_shapes=[
            pltpu.SMEM(band_table.shape, jnp.int32),
            pltpu.SMEM(windows.shape, jnp.int32),
            pltpu.VMEM((2, pieces, n, 4, slab, HEAD), jnp.bfloat16),
            pltpu.VMEM((2, 2, n, length, HEAD), jnp.bfloat16),
            pltpu.VMEM(out_weight.shape, jnp.bfloat16),
            pltpu.VMEM((2, pieces, n, 4 * slab, HEAD), jnp.bfloat16),
            pltpu.VMEM((pieces, 4 * slab, width), jnp.bfloat16),
            pltpu.VMEM((pieces, chunks, 2 * slab, part), jnp.bfloat16),
            pltpu.VMEM((pieces, chunks, 2 * slab, part), jnp.bfloat16),
            pltpu.VMEM((pieces, chunks, slab, part), jnp.bfloat16),
            pltpu.VMEM((pieces, chunks, slab, part), jnp.bfloat16),
            pltpu.VMEM((pieces, chunks, slab, part), jnp.float32),
            pltpu.VMEM((chunks, 2 * slab, part), jnp.float32),
            dma((heads, 2 + pieces)),
            dma((2, 2 + pieces, n)),
            dma((2, pieces, n)),
            dma((pieces, heads)),
            dma((pieces, chunks)),
            dma((pieces, chunks)),
            dma((pieces, chunks)),
            dma((pieces, chunks)),
            dma,
            dma((2,)),
        ],
        compiler_params=pltpu.CompilerParams(
            collective_id=0, has_side_effects=True, vmem_limit_bytes=60 * 1024 * 1024
        ),
    )(queries.reshape(4, block, width), keys, values, band_table, windows, out_weight)
    return mixed[None]


def solution(mesh):
    n = mesh.shape["tm"]

    def step(queries, keys, values, band_table, windows, out_weight):
        paired = mesh.shape["head"] == 2 and mesh.shape["sub"] == 2
        if n > 2 and paired and queries.shape[0] == 1 and queries.shape[2] == (2 * n - 2) * HEAD:
            return fused(n, queries, keys, values, band_table, windows, out_weight)
        return local(queries, keys, values, band_table, windows, out_weight)

    return jax.shard_map(
        step,
        mesh=mesh,
        in_specs=(
            P(("clip", "tm"), None, ("head", "sub")),
            P(("clip", "tm"), None, ("head", "sub")),
            P(("clip", "tm"), None, ("head", "sub")),
            P(),
            P(),
            P(("head", "sub"), None),
        ),
        out_specs=P(("clip", "tm"), ("head", "sub"), None),
        check_vma=False,
    )
```

profile of v0, /device:TPU:0, one launch (start us, length us, event | category | flops | bytes accessed | tf_op | source)
XLA Modules:
  0.0 51.9 jit_solution(1007402802743960783)
XLA Ops:
  0.0 50.2 %shard_map.64 = bf16[64,3072]{1,0:T(8,128)(2,1)} custom-call(bf16[4,64,768]{2,1,0:T(8,128)(2,1)} %bitcast.3, bf16[1,256,768]{2,1,0:T(8,128)(2,1)} %k_hbm.1, bf16[1,256,768]{2,1,0:T(8,128)(2,1)} %v_hbm.1, s32[4,4]{1,0:T(4,128)} %band_hbm.1, s32[7]{0:T(128)} %windows_hbm.1, bf16[768,3072]{1,0:T(8,128)(2,1)} %w_hbm.1), custom_call_target="tpu_custom_call" | custom-call | tf_op jit(solution)/shard_map/pallas_call | solution.py:337
  50.2 1.8 %copy.8 = bf16[1,64,3072]{2,1,0:T(8,128)(2,1)} copy(bf16[1,64,3072]{2,1,0:T(8,128)(2,1)} %bitcast.2) | data formatting | bytes 786432
where the time goes:
time: 52.1 us; the launch traced here: 51.9 us
  Pallas kernels  50.2 us (96%)
  local copies, waits for them, and re-layouts  1.77 us (3%)
    pallas_call x1, Pallas kernels, fused(): pl.pallas_call(functools.partial(fused_kernel, n, pieces, chunks), out_sh...  50.2 us
    unnamed x1, local copies, waits for them, and re-layouts  1.77 us

commit v1 on v0

v1 whole, which is shorter than its diff:
```python
import functools
import math

import jax
import jax.numpy as jnp
from jax import lax
from jax.experimental import pallas as pl
from jax.experimental.pallas import tpu as pltpu
from jax.sharding import PartitionSpec as P

HEAD = 128
MESH = pl.DeviceIdType.MESH


def local(queries, keys, values, band_table, windows, out_weight):
    frames, length, width = queries.shape
    heads = width // HEAD
    scale = HEAD ** (-0.5)
    here = lax.axis_index("tm") * frames
    query = queries[0].reshape(length, heads, HEAD)
    places = lax.iota(jnp.int32, length)
    gap = jnp.abs(places[:, None] - places[None, :])

    def absorb(carry, key_frame, value_frame, frame, usable):
        peak, total, numer = carry
        reach = windows[band_table[here, frame]]
        allowed = (gap <= reach)[None] & usable
        scores = (
            jnp.einsum(
                "phd,qhd->hpq",
                query,
                key_frame.reshape(length, heads, HEAD),
                preferred_element_type=jnp.float32,
            )
            * scale
        )
        masked = jnp.where(allowed, scores, jnp.float32(-1e30))
        top = jnp.maximum(peak, jnp.max(masked, axis=-1))
        weights = jnp.where(allowed, jnp.exp(scores - top[:, :, None]), jnp.float32(0.0))
        shrink = jnp.exp(peak - top)
        total = total * shrink + jnp.sum(weights, axis=-1)
        added = jnp.einsum(
            "hpq,qhd->phd",
            weights.astype(jnp.bfloat16),
            value_frame.reshape(length, heads, HEAD),
            preferred_element_type=jnp.float32,
        )
        numer = numer * jnp.transpose(shrink)[:, :, None] + added
        return (top, total, numer)

    carry = (
        jnp.full((heads, length), -1e30, jnp.float32),
        jnp.zeros((heads, length), jnp.float32),
        jnp.zeros((length, heads, HEAD), jnp.float32),
    )
    skipped = -1
    state = carry
    key_part = lax.all_gather(keys, "tm", axis=0, tiled=True)
    value_part = lax.all_gather(values, "tm", axis=0, tiled=True)

    def advance(inner, item):
        key_frame, value_frame, offset = item
        usable = jnp.abs(offset - here) > skipped
        return (absorb(inner, key_frame, value_frame, offset, usable), None)

    state, unused = lax.scan(
        advance, state, (key_part, value_part, lax.iota(jnp.int32, key_part.shape[0]))
    )
    carry = state
    peak, total, numer = carry
    attended = (
        (numer / jnp.transpose(total)[:, :, None]).astype(jnp.bfloat16).reshape(length, width)
    )
    mixed = lax.psum_scatter(
        jnp.dot(attended, out_weight, preferred_element_type=jnp.float32).astype(jnp.bfloat16),
        ("head", "sub"),
        scatter_dimension=0,
        tiled=True,
    )
    return mixed[None]


def fused_kernel(
    n, pieces, chunks, q_hbm, k_hbm, v_hbm, band_hbm, windows_hbm, w_hbm, out_ref,
    band, windows, asked_a, asked_b, buf, weight, done_a, done_b, att,
    send_a, recv_a, send_b, recv_b, acc, own, known,
    in_send, in_recv_a, in_recv_b, back_send_a, back_recv_a, back_send_b, back_recv_b,
    a_send, a_recv, b_send, b_recv, w_sem, table_sem,
):
    frame = lax.axis_index("tm")
    row = lax.axis_index("head")
    core = lax.axis_index("sub")
    length = k_hbm.shape[1]
    block = length // 4
    slab = block // pieces
    heads = 2 * n - 2
    half = n // 2
    owner = [(h + 1) // 2 for h in range(heads)]
    slot = [1 if h > 0 and h % 2 == 0 else 0 for h in range(heads)]
    factor = HEAD ** (-0.5) * math.log2(math.e)
    ahead = min(2, pieces)

    def inner(z):
        return z + 1 if z < half else z - 1

    def outward(z):
        return list(range(z - 1, -1, -1)) if z < half else list(range(z + 1, n))

    def beyond(z):
        return list(range(z + 2, n)) if z < half else list(range(z - 2, -1, -1))

    def owned(z, s):
        return [h for h in range(heads) if owner[h] == z and slot[h] == s]

    def ends(h, a):
        columns = slice(h * HEAD, (h + 1) * HEAD)
        if a < 2:
            return (k_hbm, v_hbm)[a].at[0, :, columns], buf.at[slot[h], a, frame]
        if slot[h]:
            return q_hbm.at[:, :, columns], asked_a.at[frame]
        p = a - 2
        return q_hbm.at[:, p * slab : (p + 1) * slab, columns], asked_b.at[p, frame]

    def landed(h, a):
        return (in_recv_a if slot[h] else in_recv_b).at[a, frame]

    def parts_of(h):
        return 3 if slot[h] else 2 + pieces

    def outgoing(h, a):
        source, target = ends(h, a)
        return pltpu.make_async_remote_copy(
            src_ref=source,
            dst_ref=target,
            send_sem=in_send.at[h, a],
            recv_sem=landed(h, a),
            device_id={"tm": owner[h]},
            device_id_type=MESH,
        )

    def send(some):
        for h in some:
            for a in (0, 2, 1) if slot[h] else (0, 2, 1, *range(3, 2 + ahead)):
                outgoing(h, a).start()

    def tell(z, w):
        pl.semaphore_signal(known.at[w], inc=1, device_id={"tm": z}, device_id_type=MESH)

    def enter(z):
        barrier = pltpu.get_barrier_semaphore()
        middle = z in (half - 1, half)
        out = outward(z)
        for w in ([inner(z)] if middle else []) + out[:1]:
            pl.semaphore_signal(barrier, inc=1, device_id={"tm": w}, device_id_type=MESH)
        pl.semaphore_signal(barrier, inc=1, device_id={"head": 1 - row}, device_id_type=MESH)
        pl.semaphore_signal(barrier, inc=1, device_id={"sub": 1 - core}, device_id_type=MESH)
        pl.semaphore_wait(barrier, 3)
        if not middle:
            tell(inner(z), z)
        send(owned(inner(z), 1))
        if middle:
            send(owned(inner(z), 0))
        for w in out:
            pl.semaphore_wait(known.at[w], 1)
            tell(inner(z), w)
            if w == out[0]:
                tell(w, inner(z))
            send(owned(w, 1) + owned(w, 0))
        for w in beyond(z):
            pl.semaphore_wait(known.at[w], 1)
            if out:
                tell(out[0], w)
            send(owned(w, 1) + owned(w, 0))
        if not middle:
            send(owned(inner(z), 0))
        for h in owned(z, 1) + owned(z, 0):
            for a in range(parts_of(h)):
                source, target = ends(h, a)
                pltpu.make_async_copy(source, target, landed(h, a)).start()

    for z in range(n):
        @pl.when(frame == z)
        def _():
            enter(z)

    load_weight = pltpu.make_async_copy(w_hbm, weight, w_sem)
    load_weight.start()
    tables = (
        pltpu.make_async_copy(band_hbm, band, table_sem.at[0]),
        pltpu.make_async_copy(windows_hbm, windows, table_sem.at[1]),
    )
    for table in tables:
        table.start()
    for table in tables:
        table.wait()

    def returning_a(h, i):
        return pltpu.make_async_remote_copy(
            src_ref=done_a.at[i],
            dst_ref=att.at[:, :, pl.ds(pl.multiple_of(h * HEAD, HEAD), HEAD)],
            send_sem=back_send_a.at[i],
            recv_sem=back_recv_a.at[h],
            device_id={"tm": i},
            device_id_type=MESH,
        )

    def returning_b(h, p, i):
        return pltpu.make_async_remote_copy(
            src_ref=done_b.at[p, i],
            dst_ref=att.at[
                :, p * slab : (p + 1) * slab, pl.ds(pl.multiple_of(h * HEAD, HEAD), HEAD)
            ],
            send_sem=back_send_b.at[p, i],
            recv_sem=back_recv_b.at[p, h],
            device_id={"tm": i},
            device_id_type=MESH,
        )

    def weigh(s, query, masked):
        scores = []
        for j in range(n):
            score = lax.dot_general(
                query, buf[s, 0, j], (((1,), (1,)), ((), ())), preferred_element_type=jnp.float32
            )
            scores.append(masked(j, score))
        top = scores[0]
        for score in scores[1:]:
            top = jnp.maximum(top, score)
        top = jnp.max(top, axis=-1, keepdims=True)
        total = None
        numer = None
        for j in range(n):
            part = jnp.exp2((scores[j] - top) * factor)
            product = jnp.dot(
                part.astype(jnp.bfloat16), buf[s, 1, j], preferred_element_type=jnp.float32
            )
            total = part if total is None else total + part
            numer = product if numer is None else numer + product
        return (numer / jnp.sum(total, axis=-1, keepdims=True)).astype(jnp.bfloat16)

    second = 2 * frame
    first = 2 * frame - (frame + n - 1) // n
    both = jnp.logical_and(frame > 0, frame < n - 1)
    column = lax.broadcasted_iota(jnp.int32, (length, length), 1)
    gap_a = jnp.abs(lax.broadcasted_iota(jnp.int32, (length, length), 0) - column)

    @pl.when(both)
    def _():
        for j in range(n):
            for a in range(2):
                here = buf.at[1, a, j]
                pltpu.make_async_copy(here, here, in_recv_a.at[a, j]).wait()
            here = asked_a.at[j]
            pltpu.make_async_copy(here, here, in_recv_a.at[2, j]).wait()

        def one(step, carry):
            i = lax.rem(frame + 1 + step, n)

            def masked(j, score):
                return jnp.where(gap_a <= windows[band[i, j]], score, jnp.float32(-1e30))

            result = weigh(1, asked_a[i].reshape(length, HEAD), masked)
            result = result.reshape(4, block, HEAD)

            @pl.when(i != frame)
            def _():
                done_a[i] = result
                returning_a(second, i).start()

            @pl.when(i == frame)
            def _():
                att[:, :, pl.ds(pl.multiple_of(second * HEAD, HEAD), HEAD)] = result

            return carry

        lax.fori_loop(0, n, one, 0)

    height = 4 * slab
    spot = lax.broadcasted_iota(jnp.int32, (height, length), 0)
    spot = (spot // slab) * block + lax.rem(spot, slab)
    spot = spot - lax.broadcasted_iota(jnp.int32, (height, length), 1)

    def more(p):
        for z in range(n):
            @pl.when(frame == z)
            def _():
                for w in beyond(z)[::-1] + outward(z) + [inner(z)]:
                    for h in owned(w, 0):
                        outgoing(h, 2 + p).start()

    def attend(p):
        for j in range(n):
            for a in range(2) if p == 0 else ():
                here = buf.at[0, a, j]
                pltpu.make_async_copy(here, here, in_recv_b.at[a, j]).wait()
            here = asked_b.at[p, j]
            pltpu.make_async_copy(here, here, in_recv_b.at[2 + p, j]).wait()
        gap = jnp.abs(spot + p * slab)

        def masked(j, score):
            return jnp.concatenate(
                [
                    jnp.where(
                        gap <= windows[band[i, j]],
                        score[i * height : (i + 1) * height],
                        jnp.float32(-1e30),
                    )
                    for i in range(n)
                ],
                axis=0,
            )

        result = weigh(0, asked_b[p].reshape(n * height, HEAD), masked)
        for i in range(n):
            mine = result[i * height : (i + 1) * height].reshape(4, slab, HEAD)

            @pl.when(i != frame)
            def _():
                done_b[p, i] = mine
                returning_b(first, p, i).start()

            @pl.when(i == frame)
            def _():
                att[
                    :, p * slab : (p + 1) * slab, pl.ds(pl.multiple_of(first * HEAD, HEAD), HEAD)
                ] = mine

    width = weight.shape[1] // chunks

    def give_a(p, c):
        return pltpu.make_async_remote_copy(
            src_ref=send_a.at[p, c], dst_ref=recv_a.at[p, c],
            send_sem=a_send.at[p, c], recv_sem=a_recv.at[p, c],
            device_id={"sub": 1 - core}, device_id_type=MESH,
        )

    def give_b(p, c):
        return pltpu.make_async_remote_copy(
            src_ref=send_b.at[p, c], dst_ref=recv_b.at[p, c],
            send_sem=b_send.at[p, c], recv_sem=b_recv.at[p, c],
            device_id={"head": 1 - row}, device_id_type=MESH,
        )

    def project(p):
        for h in range(heads):
            if slot[h] and p > 0:
                continue

            @pl.when(frame != owner[h])
            def _():
                columns = slice(h * HEAD, (h + 1) * HEAD)
                if slot[h]:
                    here = att.at[:, :, columns]
                    pltpu.make_async_copy(here, here, back_recv_a.at[h]).wait()
                else:
                    here = att.at[:, p * slab : (p + 1) * slab, columns]
                    pltpu.make_async_copy(here, here, back_recv_b.at[p, h]).wait()

        tokens = jnp.concatenate(
            [
                att[r * 2 + who, p * slab : (p + 1) * slab, :]
                for who in (1 - core, core)
                for r in (row, 1 - row)
            ],
            axis=0,
        )
        for c in range(chunks):
            share = jnp.dot(
                tokens, weight[:, c * width : (c + 1) * width], preferred_element_type=jnp.float32
            )
            send_a[p, c] = share[: 2 * slab].astype(jnp.bfloat16)
            give_a(p, c).start()
            own[c] = share[2 * slab :]

    def pair(p):
        for c in range(chunks):
            give_a(p, c).wait_recv()
            both_cores = own[c] + recv_a[p, c].astype(jnp.float32)
            send_b[p, c] = both_cores[slab:].astype(jnp.bfloat16)
            give_b(p, c).start()
            acc[p, c] = both_cores[:slab]

    def finish(p):
        for c in range(chunks):
            give_b(p, c).wait_recv()
            out_ref[p * slab : (p + 1) * slab, c * width : (c + 1) * width] = (
                acc[p, c] + recv_b[p, c].astype(jnp.float32)
            ).astype(jnp.bfloat16)

    for p in range(pieces):
        if p + ahead < pieces:
            more(p + ahead)
        attend(p)
        if p == 1:
            load_weight.wait()
        if p > 1:
            pair(p - 2)
        if p > 0:
            project(p - 1)
    pair(pieces - 2)
    for p in range(pieces - 2):
        finish(p)
    project(pieces - 1)
    finish(pieces - 2)
    pair(pieces - 1)
    finish(pieces - 1)

    for p in range(pieces):
        for c in range(chunks):
            give_a(p, c).wait_send()
            give_b(p, c).wait_send()
    for h in range(heads):

        @pl.when(frame != owner[h])
        def _():
            for a in range(parts_of(h)):
                outgoing(h, a).wait_send()

    for i in range(n):

        @pl.when(i != frame)
        def _():
            for p in range(pieces):
                returning_b(first, p, i).wait_send()

        @pl.when(jnp.logical_and(both, i != frame))
        def _():
            returning_a(second, i).wait_send()


def fused(n, queries, keys, values, band_table, windows, out_weight):
    length, width = queries.shape[1:]
    columns = out_weight.shape[1]
    heads = width // HEAD
    block = length // 4
    chunks = 2
    pieces = 4
    slab = block // pieces
    part = columns // chunks
    anywhere = pl.BlockSpec(memory_space=pl.ANY)
    dma = pltpu.SemaphoreType.DMA
    arrays = (queries.reshape(4, block, width), keys, values, band_table, windows, out_weight)
    mixed = pl.pallas_call(
        functools.partial(fused_kernel, n, pieces, chunks),
        out_shape=pltpu.VMEM((block, columns), jnp.bfloat16),
        in_specs=[anywhere] * 6,
        out_specs=pl.BlockSpec(memory_space=pltpu.VMEM),
        scratch_shapes=[
            pltpu.SMEM(band_table.shape, jnp.int32),
            pltpu.SMEM(windows.shape, jnp.int32),
            pltpu.VMEM((n, 4, block, HEAD), jnp.bfloat16),
            pltpu.VMEM((pieces, n, 4, slab, HEAD), jnp.bfloat16),
            pltpu.VMEM((2, 2, n, length, HEAD), jnp.bfloat16),
            pltpu.VMEM(out_weight.shape, jnp.bfloat16),
            pltpu.VMEM((n, 4, block, HEAD), jnp.bfloat16),
            pltpu.VMEM((pieces, n, 4, slab, HEAD), jnp.bfloat16),
            pltpu.VMEM((4, block, width), jnp.bfloat16),
            pltpu.VMEM((pieces, chunks, 2 * slab, part), jnp.bfloat16),
            pltpu.VMEM((pieces, chunks, 2 * slab, part), jnp.bfloat16),
            pltpu.VMEM((pieces, chunks, slab, part), jnp.bfloat16),
            pltpu.VMEM((pieces, chunks, slab, part), jnp.bfloat16),
            pltpu.VMEM((pieces, chunks, slab, part), jnp.float32),
            pltpu.VMEM((chunks, 2 * slab, part), jnp.float32),
            pltpu.SemaphoreType.REGULAR((n,)),
            dma((heads, 2 + pieces)),
            dma((3, n)),
            dma((2 + pieces, n)),
            dma((n,)),
            dma((heads,)),
            dma((pieces, n)),
            dma((pieces, heads)),
            dma((pieces, chunks)),
            dma((pieces, chunks)),
            dma((pieces, chunks)),
            dma((pieces, chunks)),
            dma,
            dma((2,)),
        ],
        compiler_params=pltpu.CompilerParams(
            collective_id=0, has_side_effects=True, vmem_limit_bytes=60 * 1024 * 1024
        ),
    )(*[pltpu.with_memory_space_constraint(x, pltpu.HBM) for x in arrays])
    return mixed[None]


def solution(mesh):
    n = mesh.shape["tm"]

    def step(queries, keys, values, band_table, windows, out_weight):
        paired = mesh.shape["head"] == 2 and mesh.shape["sub"] == 2
        fits = queries.shape[0] == 1 and queries.shape[1] % 256 == 0
        if n > 2 and paired and fits and queries.shape[2] == (2 * n - 2) * HEAD:
            return fused(n, queries, keys, values, band_table, windows, out_weight)
        return local(queries, keys, values, band_table, windows, out_weight)

    return jax.shard_map(
        step,
        mesh=mesh,
        in_specs=(
            P(("clip", "tm"), None, ("head", "sub")),
            P(("clip", "tm"), None, ("head", "sub")),
            P(("clip", "tm"), None, ("head", "sub")),
            P(),
            P(),
            P(("head", "sub"), None),
        ),
        out_specs=P(("clip", "tm"), ("head", "sub"), None),
        check_vma=False,
    )
```

time: 52.1 us -> 53.5 us (1.027)
  Pallas kernels: 50.2 us -> 52.6 us
  local copies, waits for them, and re-layouts: 1.77 us -> 0.75 us
    pallas_call x1, Pallas kernels: 50.2 us -> 52.6 us  [fused(): pl.pallas_call(functools.partial(fused_kernel, n, pieces, chunks), out_sh...]
    unnamed x1, local copies, waits for them, and re-layouts: 1.77 us -> 0.75 us
where the time goes in v1:
time: 53.5 us; the launch traced here: 53.3 us
  Pallas kernels  52.6 us (98%)
  local copies, waits for them, and re-layouts  0.75 us (1%)
    pallas_call x1, Pallas kernels, fused(): pl.pallas_call(functools.partial(fused_kernel, n, pieces, chunks), out_sh...  52.6 us

profile of v1, /device:TPU:0, one launch (start us, length us, event | category | flops | bytes accessed | tf_op | source)
XLA Modules:
  0.0 53.3 jit_solution(436558586354319487)
XLA Ops:
  0.0 52.6 %shard_map.64 = bf16[64,3072]{1,0:T(8,128)(2,1)S(1)} custom-call(bf16[4,64,768]{2,1,0:T(8,128)(2,1)} %bitcast.3, bf16[1,256,768]{2,1,0:T(8,128)(2,1)} %k_hbm.1, bf16[1,256,768]{2,1,0:T(8,128)(2,1)} %v_hbm.1, s32[4,4]{1,0:T(4,128)} %band_hbm.1, s32[7]{0:T(128)} %windows_hbm.1, bf16[768,3072]{1,0:T(8,128)(2,1)} %w_hbm.1), custom_call_target="tpu_custom_call" | custom-call | tf_op jit(solution)/shard_map/pallas_call | solution.py:443
  52.6 0.7 %copy.8 = bf16[1,64,3072]{2,1,0:T(8,128)(2,1)} copy(bf16[1,64,3072]{2,1,0:T(8,128)(2,1)S(1)} %bitcast.2) | data formatting | bytes 786432

commit v2 on v1

v2 whole, which is shorter than its diff:
```python
import functools
import math

import jax
import jax.numpy as jnp
from jax import lax
from jax.experimental import pallas as pl
from jax.experimental.pallas import tpu as pltpu
from jax.sharding import PartitionSpec as P

HEAD = 128
MESH = pl.DeviceIdType.MESH


def local(queries, keys, values, band_table, windows, out_weight):
    frames, length, width = queries.shape
    heads = width // HEAD
    scale = HEAD ** (-0.5)
    here = lax.axis_index("tm") * frames
    query = queries[0].reshape(length, heads, HEAD)
    places = lax.iota(jnp.int32, length)
    gap = jnp.abs(places[:, None] - places[None, :])

    def absorb(carry, key_frame, value_frame, frame, usable):
        peak, total, numer = carry
        reach = windows[band_table[here, frame]]
        allowed = (gap <= reach)[None] & usable
        scores = (
            jnp.einsum(
                "phd,qhd->hpq",
                query,
                key_frame.reshape(length, heads, HEAD),
                preferred_element_type=jnp.float32,
            )
            * scale
        )
        masked = jnp.where(allowed, scores, jnp.float32(-1e30))
        top = jnp.maximum(peak, jnp.max(masked, axis=-1))
        weights = jnp.where(allowed, jnp.exp(scores - top[:, :, None]), jnp.float32(0.0))
        shrink = jnp.exp(peak - top)
        total = total * shrink + jnp.sum(weights, axis=-1)
        added = jnp.einsum(
            "hpq,qhd->phd",
            weights.astype(jnp.bfloat16),
            value_frame.reshape(length, heads, HEAD),
            preferred_element_type=jnp.float32,
        )
        numer = numer * jnp.transpose(shrink)[:, :, None] + added
        return (top, total, numer)

    carry = (
        jnp.full((heads, length), -1e30, jnp.float32),
        jnp.zeros((heads, length), jnp.float32),
        jnp.zeros((length, heads, HEAD), jnp.float32),
    )
    skipped = -1
    state = carry
    key_part = lax.all_gather(keys, "tm", axis=0, tiled=True)
    value_part = lax.all_gather(values, "tm", axis=0, tiled=True)

    def advance(inner, item):
        key_frame, value_frame, offset = item
        usable = jnp.abs(offset - here) > skipped
        return (absorb(inner, key_frame, value_frame, offset, usable), None)

    state, unused = lax.scan(
        advance, state, (key_part, value_part, lax.iota(jnp.int32, key_part.shape[0]))
    )
    carry = state
    peak, total, numer = carry
    attended = (
        (numer / jnp.transpose(total)[:, :, None]).astype(jnp.bfloat16).reshape(length, width)
    )
    mixed = lax.psum_scatter(
        jnp.dot(attended, out_weight, preferred_element_type=jnp.float32).astype(jnp.bfloat16),
        ("head", "sub"),
        scatter_dimension=0,
        tiled=True,
    )
    return mixed[None]


def fused_kernel(
    n, chunks, q_hbm, k_hbm, v_hbm, band_hbm, windows_hbm, w_hbm, out_ref,
    band, windows, asked, buf, weight, done, att, send_a, recv_a, send_b, recv_b, own, known,
    in_send, in_recv, back_send, back_recv, a_send, a_recv, b_send, b_recv, w_sem, table_sem,
):
    frame = lax.axis_index("tm")
    row = lax.axis_index("head")
    core = lax.axis_index("sub")
    length = k_hbm.shape[1]
    block = length // 4
    slab = block // 2
    pieces = 4
    heads = 2 * n - 2
    half = n // 2
    owner = [(h + 1) // 2 for h in range(heads)]
    slot = [1 if h > 0 and h % 2 == 0 else 0 for h in range(heads)]
    factor = HEAD ** (-0.5) * math.log2(math.e)
    ahead = 2

    def inner(z):
        return z + 1 if z < half else z - 1

    def outward(z):
        return list(range(z - 1, -1, -1)) if z < half else list(range(z + 1, n))

    def beyond(z):
        return list(range(z + 2, n)) if z < half else list(range(z - 2, -1, -1))

    def owned(z):
        return [h for h in range(heads) if owner[h] == z and slot[h]] + [
            h for h in range(heads) if owner[h] == z and not slot[h]
        ]

    def piece(ref, p, columns):
        if p < 2:
            return ref.at[pl.ds(2 * (1 - row), 2), p, :, columns]
        return ref.at[2 * row + (1 - core if p == 2 else core), :, :, columns]

    def ends(h, a):
        columns = slice(h * HEAD, (h + 1) * HEAD)
        if a < 2:
            return (k_hbm, v_hbm)[a].at[0, :, columns], buf.at[slot[h], a, frame]
        return piece(q_hbm, a - 2, columns), asked.at[slot[h], a - 2, frame]

    def outgoing(h, a):
        source, target = ends(h, a)
        return pltpu.make_async_remote_copy(
            src_ref=source,
            dst_ref=target,
            send_sem=in_send.at[h, a],
            recv_sem=in_recv.at[slot[h], a, frame],
            device_id={"tm": owner[h]},
            device_id_type=MESH,
        )

    def give(some):
        for h in some:
            for a in range(2):
                outgoing(h, a).start()

    def ask(z, p):
        near = [inner(z)] if z in (half - 1, half) else []
        far = [inner(z)] if z not in (half - 1, half) else []
        for w in near + beyond(z) + far + outward(z):
            for h in owned(w):
                outgoing(h, 2 + p).start()

    def tell(z, w):
        pl.semaphore_signal(known.at[w], inc=1, device_id={"tm": z}, device_id_type=MESH)

    def enter(z):
        barrier = pltpu.get_barrier_semaphore()
        middle = z in (half - 1, half)
        out = outward(z)
        for w in ([inner(z)] if middle else []) + out[:1]:
            pl.semaphore_signal(barrier, inc=1, device_id={"tm": w}, device_id_type=MESH)
        pl.semaphore_signal(barrier, inc=1, device_id={"head": 1 - row}, device_id_type=MESH)
        pl.semaphore_signal(barrier, inc=1, device_id={"sub": 1 - core}, device_id_type=MESH)
        pl.semaphore_wait(barrier, 3)
        if not middle:
            tell(inner(z), z)
        close = owned(inner(z))
        if middle:
            give(close)
        else:
            outgoing(close[0], 0).start()
        for w in out:
            pl.semaphore_wait(known.at[w], 1)
            tell(inner(z), w)
            if w == out[0]:
                tell(w, inner(z))
            give(owned(w))
        for w in beyond(z):
            pl.semaphore_wait(known.at[w], 1)
            if out:
                tell(out[0], w)
            give(owned(w))
        if not middle:
            outgoing(close[0], 1).start()
            give(close[1:])
        ask(z, 0)

        @pl.when(core == 0)
        def _():
            for p in range(1, ahead):
                ask(z, p)

        for h in owned(z):
            for a in range(2 + pieces):
                source, target = ends(h, a)
                pltpu.make_async_copy(source, target, in_recv.at[slot[h], a, frame]).start()

    for z in range(n):
        @pl.when(frame == z)
        def _():
            enter(z)

    load_weight = pltpu.make_async_copy(w_hbm, weight, w_sem)
    load_weight.start()
    tables = (
        pltpu.make_async_copy(band_hbm, band, table_sem.at[0]),
        pltpu.make_async_copy(windows_hbm, windows, table_sem.at[1]),
    )
    for table in tables:
        table.start()
    for table in tables:
        table.wait()

    def returning(s, h, p, i):
        return pltpu.make_async_remote_copy(
            src_ref=done.at[s, p, i],
            dst_ref=piece(att, p, pl.ds(pl.multiple_of(h * HEAD, HEAD), HEAD)),
            send_sem=back_send.at[s, p, i],
            recv_sem=back_recv.at[p, h],
            device_id={"tm": i},
            device_id_type=MESH,
        )

    def weigh(s, query, masked):
        scores = []
        for j in range(n):
            score = lax.dot_general(
                query, buf[s, 0, j], (((1,), (1,)), ((), ())), preferred_element_type=jnp.float32
            )
            scores.append(masked(j, score))
        top = scores[0]
        for score in scores[1:]:
            top = jnp.maximum(top, score)
        top = jnp.max(top, axis=-1, keepdims=True)
        total = None
        numer = None
        for j in range(n):
            part = jnp.exp2((scores[j] - top) * factor)
            product = jnp.dot(
                part.astype(jnp.bfloat16), buf[s, 1, j], preferred_element_type=jnp.float32
            )
            total = part if total is None else total + part
            numer = product if numer is None else numer + product
        return (numer / jnp.sum(total, axis=-1, keepdims=True)).astype(jnp.bfloat16)

    second = 2 * frame
    first = 2 * frame - (frame + n - 1) // n
    both = jnp.logical_and(frame > 0, frame < n - 1)
    height = 2 * slab
    line = lax.broadcasted_iota(jnp.int32, (height, length), 0)
    column = lax.broadcasted_iota(jnp.int32, (height, length), 1)

    def away(p):
        if p < 2:
            spot = (line // slab) * block + lax.rem(line, slab)
            start = 2 * (1 - row) * block + p * slab
        else:
            spot = line
            start = (2 * row + (1 - core if p == 2 else core)) * block
        return jnp.abs(spot - column + start)

    def more(p):
        for z in range(n):
            @pl.when(frame == z)
            def _():
                ask(z, p)

    def arrive(s, p):
        for j in range(n):
            for a in range(2) if p == 0 else ():
                here = buf.at[s, a, j]
                pltpu.make_async_copy(here, here, in_recv.at[s, a, j]).wait()
            here = asked.at[s, p, j]
            pltpu.make_async_copy(here, here, in_recv.at[s, 2 + p, j]).wait()

    def attend(s, h, p):
        gap = away(p)

        def masked(j, score):
            return jnp.concatenate(
                [
                    jnp.where(
                        gap <= windows[band[i, j]],
                        score[i * height : (i + 1) * height],
                        jnp.float32(-1e30),
                    )
                    for i in range(n)
                ],
                axis=0,
            )

        result = weigh(s, asked[s, p].reshape(n * height, HEAD), masked)
        for i in range(n):
            mine = result[i * height : (i + 1) * height].reshape(2, slab, HEAD)

            @pl.when(i != frame)
            def _():
                done[s, p, i] = mine
                returning(s, h, p, i).start()

            @pl.when(i == frame)
            def _():
                piece(att, p, pl.ds(pl.multiple_of(h * HEAD, HEAD), HEAD))[...] = mine

    width = weight.shape[1] // chunks

    def give_a(p, c):
        lines = slice(0, slab if p < 2 else block)
        return pltpu.make_async_remote_copy(
            src_ref=send_a.at[p, c, lines], dst_ref=recv_a.at[p, c, lines],
            send_sem=a_send.at[p, c], recv_sem=a_recv.at[p, c],
            device_id={"sub": 1 - core}, device_id_type=MESH,
        )

    def give_b(p, c):
        return pltpu.make_async_remote_copy(
            src_ref=send_b.at[p, c], dst_ref=recv_b.at[p, c],
            send_sem=b_send.at[p, c], recv_sem=b_recv.at[p, c],
            device_id={"head": 1 - row}, device_id_type=MESH,
        )

    def returned(p):
        for h in range(heads):

            @pl.when(frame != owner[h])
            def _():
                here = piece(att, p, slice(h * HEAD, (h + 1) * HEAD))
                pltpu.make_async_copy(here, here, back_recv.at[p, h]).wait()

    def share(tokens, c):
        return jnp.dot(
            tokens, weight[:, c * width : (c + 1) * width], preferred_element_type=jnp.float32
        )

    def project(p):
        returned(p)
        if p < 2:
            tokens = jnp.concatenate(
                [att[2 * (1 - row) + who, p] for who in (1 - core, core)], axis=0
            )
        else:
            tokens = att[2 * row + (1 - core if p == 2 else core)].reshape(block, heads * HEAD)
        for c in range(chunks):
            part = share(tokens, c)
            if p < 2:
                send_a[p, c, :slab] = part[:slab].astype(jnp.bfloat16)
                own[p, c] = part[slab:]
            elif p == 2:
                send_a[p, c] = part.astype(jnp.bfloat16)
            if p < 3:
                give_a(p, c).start()
            else:
                give_a(2, c).wait_recv()
                part = part + recv_a[2, c].astype(jnp.float32)
                for half_block in range(2):
                    lines = slice(half_block * slab, (half_block + 1) * slab)
                    give_b(half_block, c).wait_recv()
                    out_ref[lines, c * width : (c + 1) * width] = (
                        part[lines] + recv_b[half_block, c].astype(jnp.float32)
                    ).astype(jnp.bfloat16)

    def pair(p):
        for c in range(chunks):
            give_a(p, c).wait_recv()
            send_b[p, c] = (own[p, c] + recv_a[p, c, :slab].astype(jnp.float32)).astype(
                jnp.bfloat16
            )
            give_b(p, c).start()

    def work(p):
        @pl.when(both)
        def _():
            arrive(1, p)

        @pl.when(jnp.logical_not(both))
        def _():
            arrive(0, p)

        @pl.when(core == 0)
        def _():
            if p + ahead < pieces:
                more(p + ahead)

        @pl.when(core == 1)
        def _():
            if p + 1 < pieces:
                more(p + 1)

        @pl.when(both)
        def _():
            attend(1, second, p)
            arrive(0, p)

        attend(0, first, p)

    work(0)
    work(1)
    load_weight.wait()
    project(0)
    work(2)
    pair(0)
    project(1)
    pair(1)
    work(3)
    project(2)
    project(3)

    for c in range(chunks):
        for p in range(3):
            give_a(p, c).wait_send()
        for p in range(2):
            give_b(p, c).wait_send()
    for h in range(heads):

        @pl.when(frame != owner[h])
        def _():
            for a in range(2 + pieces):
                outgoing(h, a).wait_send()

    for i in range(n):

        @pl.when(i != frame)
        def _():
            for p in range(pieces):
                returning(0, first, p, i).wait_send()

        @pl.when(jnp.logical_and(both, i != frame))
        def _():
            for p in range(pieces):
                returning(1, second, p, i).wait_send()


def fused(n, queries, keys, values, band_table, windows, out_weight):
    length, width = queries.shape[1:]
    columns = out_weight.shape[1]
    heads = width // HEAD
    block = length // 4
    slab = block // 2
    chunks = 2
    pieces = 4
    part = columns // chunks
    anywhere = pl.BlockSpec(memory_space=pl.ANY)
    dma = pltpu.SemaphoreType.DMA
    arrays = (queries.reshape(4, 2, slab, width), keys, values, band_table, windows, out_weight)
    mixed = pl.pallas_call(
        functools.partial(fused_kernel, n, chunks),
        out_shape=pltpu.VMEM((block, columns), jnp.bfloat16),
        in_specs=[anywhere] * 6,
        out_specs=pl.BlockSpec(memory_space=pltpu.VMEM),
        scratch_shapes=[
            pltpu.SMEM(band_table.shape, jnp.int32),
            pltpu.SMEM(windows.shape, jnp.int32),
            pltpu.VMEM((2, pieces, n, 2, slab, HEAD), jnp.bfloat16),
            pltpu.VMEM((2, 2, n, length, HEAD), jnp.bfloat16),
            pltpu.VMEM(out_weight.shape, jnp.bfloat16),
            pltpu.VMEM((2, pieces, n, 2, slab, HEAD), jnp.bfloat16),
            pltpu.VMEM((4, 2, slab, width), jnp.bfloat16),
            pltpu.VMEM((3, chunks, block, part), jnp.bfloat16),
            pltpu.VMEM((3, chunks, block, part), jnp.bfloat16),
            pltpu.VMEM((2, chunks, slab, part), jnp.bfloat16),
            pltpu.VMEM((2, chunks, slab, part), jnp.bfloat16),
            pltpu.VMEM((2, chunks, slab, part), jnp.float32),
            pltpu.SemaphoreType.REGULAR((n,)),
            dma((heads, 2 + pieces)),
            dma((2, 2 + pieces, n)),
            dma((2, pieces, n)),
            dma((pieces, heads)),
            dma((3, chunks)),
            dma((3, chunks)),
            dma((2, chunks)),
            dma((2, chunks)),
            dma,
            dma((2,)),
        ],
        compiler_params=pltpu.CompilerParams(
            collective_id=0, has_side_effects=True, vmem_limit_bytes=60 * 1024 * 1024
        ),
    )(*[pltpu.with_memory_space_constraint(x, pltpu.HBM) for x in arrays])
    return mixed[None]


def solution(mesh):
    n = mesh.shape["tm"]

    def step(queries, keys, values, band_table, windows, out_weight):
        paired = mesh.shape["head"] == 2 and mesh.shape["sub"] == 2
        fits = queries.shape[0] == 1 and queries.shape[1] % 128 == 0
        if n > 2 and paired and fits and queries.shape[2] == (2 * n - 2) * HEAD:
            return fused(n, queries, keys, values, band_table, windows, out_weight)
        return local(queries, keys, values, band_table, windows, out_weight)

    return jax.shard_map(
        step,
        mesh=mesh,
        in_specs=(
            P(("clip", "tm"), None, ("head", "sub")),
            P(("clip", "tm"), None, ("head", "sub")),
            P(("clip", "tm"), None, ("head", "sub")),
            P(),
            P(),
            P(("head", "sub"), None),
        ),
        out_specs=P(("clip", "tm"), ("head", "sub"), None),
        check_vma=False,
    )
```

time: 53.5 us -> 45.2 us (0.84)
  Pallas kernels: 52.6 us -> 44.3 us
    pallas_call x1, Pallas kernels: 52.6 us -> 44.3 us  [fused(): pl.pallas_call(functools.partial(fused_kernel, n, chunks), out_shape=pltp...]
where the time goes in v2:
time: 45.2 us; the launch traced here: 45 us
  Pallas kernels  44.3 us (98%)
  local copies, waits for them, and re-layouts  0.75 us (2%)
    pallas_call x1, Pallas kernels, fused(): pl.pallas_call(functools.partial(fused_kernel, n, chunks), out_shape=pltp...  44.3 us

profile of v2, /device:TPU:0, one launch (start us, length us, event | category | flops | bytes accessed | tf_op | source)
XLA Modules:
  0.0 45.0 jit_solution(1613570903372452006)
XLA Ops:
  0.0 44.3 %shard_map.64 = bf16[64,3072]{1,0:T(8,128)(2,1)S(1)} custom-call(bf16[4,2,32,768]{3,2,1,0:T(8,128)(2,1)} %bitcast.3, bf16[1,256,768]{2,1,0:T(8,128)(2,1)} %k_hbm.1, bf16[1,256,768]{2,1,0:T(8,128)(2,1)} %v_hbm.1, s32[4,4]{1,0:T(4,128)} %band_hbm.1, s32[7]{0:T(128)} %windows_hbm.1, bf16[768,3072]{1,0:T(8,128)(2,1)} %w_hbm.1), custom_call_target="tpu_custom_call" | custom-call | tf_op jit(solution)/shard_map/pallas_call | solution.py:442
  44.3 0.7 %copy.8 = bf16[1,64,3072]{2,1,0:T(8,128)(2,1)} copy(bf16[1,64,3072]{2,1,0:T(8,128)(2,1)S(1)} %bitcast.2) | data formatting | bytes 786432

commit v3 on v2

--- a/solution.py
+++ b/solution.py
@@ -83,7 +83,7 @@
 def fused_kernel(
     n, chunks, q_hbm, k_hbm, v_hbm, band_hbm, windows_hbm, w_hbm, out_ref,
     band, windows, asked, buf, weight, done, att, send_a, recv_a, send_b, recv_b, own, known,
-    in_send, in_recv, back_send, back_recv, a_send, a_recv, b_send, b_recv, w_sem, table_sem,
+    in_send, in_pair, in_piece, back_send, back_recv, a_send, a_recv, b_send, b_recv, w_sem, table_sem,
 ):
     frame = lax.axis_index("tm")
     row = lax.axis_index("head")
@@ -124,13 +124,16 @@
             return (k_hbm, v_hbm)[a].at[0, :, columns], buf.at[slot[h], a, frame]
         return piece(q_hbm, a - 2, columns), asked.at[slot[h], a - 2, frame]
 
+    def landing(h, a):
+        return in_pair.at[slot[h]] if a < 2 else in_piece.at[slot[h], a - 2]
+
     def outgoing(h, a):
         source, target = ends(h, a)
         return pltpu.make_async_remote_copy(
             src_ref=source,
             dst_ref=target,
-            send_sem=in_send.at[h, a],
-            recv_sem=in_recv.at[slot[h], a, frame],
+            send_sem=in_send.at[h],
+            recv_sem=landing(h, a),
             device_id={"tm": owner[h]},
             device_id_type=MESH,
         )
@@ -190,7 +193,7 @@
         for h in owned(z):
             for a in range(2 + pieces):
                 source, target = ends(h, a)
-                pltpu.make_async_copy(source, target, in_recv.at[slot[h], a, frame]).start()
+                pltpu.make_async_copy(source, target, landing(h, a)).start()
 
     for z in range(n):
         @pl.when(frame == z)
@@ -212,8 +215,8 @@
         return pltpu.make_async_remote_copy(
             src_ref=done.at[s, p, i],
             dst_ref=piece(att, p, pl.ds(pl.multiple_of(h * HEAD, HEAD), HEAD)),
-            send_sem=back_send.at[s, p, i],
-            recv_sem=back_recv.at[p, h],
+            send_sem=back_send.at[s],
+            recv_sem=back_recv.at[p],
             device_id={"tm": i},
             device_id_type=MESH,
         )
@@ -262,13 +265,13 @@
             def _():
                 ask(z, p)
 
+    def wait_for(here, sem):
+        pltpu.make_async_copy(here, here, sem).wait()
+
     def arrive(s, p):
-        for j in range(n):
-            for a in range(2) if p == 0 else ():
-                here = buf.at[s, a, j]
-                pltpu.make_async_copy(here, here, in_recv.at[s, a, j]).wait()
-            here = asked.at[s, p, j]
-            pltpu.make_async_copy(here, here, in_recv.at[s, 2 + p, j]).wait()
+        if p == 0:
+            wait_for(buf.at[s], in_pair.at[s])
+        wait_for(asked.at[s, p], in_piece.at[s, p])
 
     def attend(s, h, p):
         gap = away(p)
@@ -305,24 +308,25 @@
         lines = slice(0, slab if p < 2 else block)
         return pltpu.make_async_remote_copy(
             src_ref=send_a.at[p, c, lines], dst_ref=recv_a.at[p, c, lines],
-            send_sem=a_send.at[p, c], recv_sem=a_recv.at[p, c],
+            send_sem=a_send, recv_sem=a_recv.at[p, c],
             device_id={"sub": 1 - core}, device_id_type=MESH,
         )
 
     def give_b(p, c):
         return pltpu.make_async_remote_copy(
             src_ref=send_b.at[p, c], dst_ref=recv_b.at[p, c],
-            send_sem=b_send.at[p, c], recv_sem=b_recv.at[p, c],
+            send_sem=b_send, recv_sem=b_recv.at[p, c],
             device_id={"head": 1 - row}, device_id_type=MESH,
         )
 
     def returned(p):
-        for h in range(heads):
-
-            @pl.when(frame != owner[h])
-            def _():
-                here = piece(att, p, slice(h * HEAD, (h + 1) * HEAD))
-                pltpu.make_async_copy(here, here, back_recv.at[p, h]).wait()
+        @pl.when(both)
+        def _():
+            wait_for(piece(att, p, slice(0, (heads - 2) * HEAD)), back_recv.at[p])
+
+        @pl.when(jnp.logical_not(both))
+        def _():
+            wait_for(piece(att, p, slice(0, (heads - 1) * HEAD)), back_recv.at[p])
 
     def share(tokens, c):
         return jnp.dot(
@@ -402,29 +406,19 @@
     project(2)
     project(3)
 
-    for c in range(chunks):
-        for p in range(3):
-            give_a(p, c).wait_send()
-        for p in range(2):
-            give_b(p, c).wait_send()
+    wait_for(send_a.at[0:2], a_send)
+    wait_for(send_b, b_send)
     for h in range(heads):
 
         @pl.when(frame != owner[h])
         def _():
-            for a in range(2 + pieces):
-                outgoing(h, a).wait_send()
-
-    for i in range(n):
-
-        @pl.when(i != frame)
-        def _():
-            for p in range(pieces):
-                returning(0, first, p, i).wait_send()
-
-        @pl.when(jnp.logical_and(both, i != frame))
-        def _():
-            for p in range(pieces):
-                returning(1, second, p, i).wait_send()
+            wait_for(buf.at[0, 0, 0:3], in_send.at[h])
+
+    wait_for(done.at[0, :, : n - 1], back_send.at[0])
+
+    @pl.when(both)
+    def _():
+        wait_for(done.at[1, :, : n - 1], back_send.at[1])
 
 
 def fused(n, queries, keys, values, band_table, windows, out_weight):
@@ -458,13 +452,14 @@
             pltpu.VMEM((2, chunks, slab, part), jnp.bfloat16),
             pltpu.VMEM((2, chunks, slab, part), jnp.float32),
             pltpu.SemaphoreType.REGULAR((n,)),
-            dma((heads, 2 + pieces)),
-            dma((2, 2 + pieces, n)),
-            dma((2, pieces, n)),
-            dma((pieces, heads)),
+            dma((heads,)),
+            dma((2,)),
+            dma((2, pieces)),
+            dma((2,)),
+            dma((pieces,)),
+            dma,
             dma((3, chunks)),
-            dma((3, chunks)),
-            dma((2, chunks)),
+            dma,
             dma((2, chunks)),
             dma,
             dma((2,)),

time: 45.2 us -> 43.9 us (0.971)
  Pallas kernels: 44.3 us -> 43 us
    pallas_call x1, Pallas kernels: 44.3 us -> 43 us  [fused(): pl.pallas_call(functools.partial(fused_kernel, n, chunks), out_shape=pltp...]
where the time goes in v3:
time: 43.9 us; the launch traced here: 43.8 us
  Pallas kernels  43 us (98%)
  local copies, waits for them, and re-layouts  0.75 us (2%)
    pallas_call x1, Pallas kernels, fused(): pl.pallas_call(functools.partial(fused_kernel, n, chunks), out_shape=pltp...  43 us

profile of v3, /device:TPU:0, one launch (start us, length us, event | category | flops | bytes accessed | tf_op | source)
XLA Modules:
  0.0 43.8 jit_solution(10716290233890006077)
XLA Ops:
  0.0 43.0 %shard_map.64 = bf16[64,3072]{1,0:T(8,128)(2,1)S(1)} custom-call(bf16[4,2,32,768]{3,2,1,0:T(8,128)(2,1)} %bitcast.3, bf16[1,256,768]{2,1,0:T(8,128)(2,1)} %k_hbm.1, bf16[1,256,768]{2,1,0:T(8,128)(2,1)} %v_hbm.1, s32[4,4]{1,0:T(4,128)} %band_hbm.1, s32[7]{0:T(128)} %windows_hbm.1, bf16[768,3072]{1,0:T(8,128)(2,1)} %w_hbm.1), custom_call_target="tpu_custom_call" | custom-call | tf_op jit(solution)/shard_map/pallas_call | solution.py:436
  43.1 0.7 %copy.8 = bf16[1,64,3072]{2,1,0:T(8,128)(2,1)} copy(bf16[1,64,3072]{2,1,0:T(8,128)(2,1)S(1)} %bitcast.2) | data formatting | bytes 786432

commit v4 on v3

--- a/solution.py
+++ b/solution.py
@@ -187,7 +187,12 @@
 
         @pl.when(core == 0)
         def _():
-            for p in range(1, ahead):
+            for p in range(1, 2 if middle else 2):
+                ask(z, p)
+
+        @pl.when(core == 1)
+        def _():
+            for p in range(1, 1 if middle else 1):
                 ask(z, p)
 
         for h in owned(z):
@@ -377,14 +382,22 @@
         def _():
             arrive(0, p)
 
-        @pl.when(core == 0)
-        def _():
-            if p + ahead < pieces:
-                more(p + ahead)
-
-        @pl.when(core == 1)
-        def _():
-            if p + 1 < pieces:
+        if p + 2 < pieces:
+
+            @pl.when((core == 0) & both)
+            def _():
+                more(p + 2)
+
+        if p + 1 < pieces:
+
+            @pl.when((core == 1) & both)
+            def _():
+                more(p + 1)
+
+        if p + 1 < pieces:
+
+            @pl.when((core == 1) & jnp.logical_not(both))
+            def _():
                 more(p + 1)
 
         @pl.when(both)
@@ -393,6 +406,12 @@
             arrive(0, p)
 
         attend(0, first, p)
+
+        if p + 2 < pieces:
+
+            @pl.when((core == 0) & jnp.logical_not(both))
+            def _():
+                more(p + 2)
 
     work(0)
     work(1)

time: 43.9 us -> 43.8 us (level)
  no operation moved by 1% of the time
where the time goes in v4:
time: 43.8 us; the launch traced here: 43.7 us
  Pallas kernels  42.9 us (98%)
  local copies, waits for them, and re-layouts  0.75 us (2%)
    pallas_call x1, Pallas kernels, fused(): pl.pallas_call(functools.partial(fused_kernel, n, chunks), out_shape=pltp...  42.9 us

profile of v4, /device:TPU:0, one launch (start us, length us, event | category | flops | bytes accessed | tf_op | source)
XLA Modules:
  0.0 43.7 jit_solution(12257036379145678559)
XLA Ops:
  0.0 42.9 %shard_map.64 = bf16[64,3072]{1,0:T(8,128)(2,1)S(1)} custom-call(bf16[4,2,32,768]{3,2,1,0:T(8,128)(2,1)} %bitcast.3, bf16[1,256,768]{2,1,0:T(8,128)(2,1)} %k_hbm.1, bf16[1,256,768]{2,1,0:T(8,128)(2,1)} %v_hbm.1, s32[4,4]{1,0:T(4,128)} %band_hbm.1, s32[7]{0:T(128)} %windows_hbm.1, bf16[768,3072]{1,0:T(8,128)(2,1)} %w_hbm.1), custom_call_target="tpu_custom_call" | custom-call | tf_op jit(solution)/shard_map/pallas_call | solution.py:455
  43.0 0.7 %copy.8 = bf16[1,64,3072]{2,1,0:T(8,128)(2,1)} copy(bf16[1,64,3072]{2,1,0:T(8,128)(2,1)S(1)} %bitcast.2) | data formatting | bytes 786432

commit v5 on v4

--- a/solution.py
+++ b/solution.py
@@ -216,12 +216,15 @@
     for table in tables:
         table.wait()
 
+    def distant(h, i):
+        return (h >= heads - 2 if i < half else h < 2).astype(jnp.int32)
+
     def returning(s, h, p, i):
         return pltpu.make_async_remote_copy(
             src_ref=done.at[s, p, i],
             dst_ref=piece(att, p, pl.ds(pl.multiple_of(h * HEAD, HEAD), HEAD)),
             send_sem=back_send.at[s],
-            recv_sem=back_recv.at[p],
+            recv_sem=back_recv.at[p if p < pieces - 1 else p + distant(h, i)],
             device_id={"tm": i},
             device_id_type=MESH,
         )
@@ -345,25 +348,54 @@
                 [att[2 * (1 - row) + who, p] for who in (1 - core, core)], axis=0
             )
         else:
-            tokens = att[2 * row + (1 - core if p == 2 else core)].reshape(block, heads * HEAD)
+            tokens = att[2 * row + 1 - core].reshape(block, heads * HEAD)
         for c in range(chunks):
             part = share(tokens, c)
             if p < 2:
                 send_a[p, c, :slab] = part[:slab].astype(jnp.bfloat16)
                 own[p, c] = part[slab:]
-            elif p == 2:
+            else:
                 send_a[p, c] = part.astype(jnp.bfloat16)
-            if p < 3:
-                give_a(p, c).start()
-            else:
-                give_a(2, c).wait_recv()
-                part = part + recv_a[2, c].astype(jnp.float32)
-                for half_block in range(2):
-                    lines = slice(half_block * slab, (half_block + 1) * slab)
-                    give_b(half_block, c).wait_recv()
-                    out_ref[lines, c * width : (c + 1) * width] = (
-                        part[lines] + recv_b[half_block, c].astype(jnp.float32)
-                    ).astype(jnp.bfloat16)
+            give_a(p, c).start()
+
+    def conclude():
+        p = pieces - 1
+
+        def gathered(heads_here, sem):
+            wait_for(piece(att, p, slice(0, heads_here * HEAD)), sem)
+
+        def term(first_head, span, c):
+            lanes = pl.ds(pl.multiple_of(first_head * HEAD, 2 * HEAD), span * HEAD)
+            return jnp.dot(
+                att[2 * row + core, :, :, lanes].reshape(block, span * HEAD),
+                weight[lanes, c * width : (c + 1) * width],
+                preferred_element_type=jnp.float32,
+            )
+
+        @pl.when(both)
+        def _():
+            gathered(heads - 4, back_recv.at[p])
+
+        @pl.when(jnp.logical_not(both))
+        def _():
+            gathered(heads - 3, back_recv.at[p])
+
+        low = frame < half
+        for c in range(chunks):
+            part = term(jnp.where(low, 0, 2), heads - 2, c)
+            give_a(2, c).wait_recv()
+            part = part + recv_a[2, c].astype(jnp.float32)
+            for half_block in range(2):
+                own[half_block, c] = part[half_block * slab : (half_block + 1) * slab]
+        gathered(2, back_recv.at[p + 1])
+        for c in range(chunks):
+            part = term(jnp.where(low, heads - 2, 0), 2, c)
+            for half_block in range(2):
+                lines = slice(half_block * slab, (half_block + 1) * slab)
+                give_b(half_block, c).wait_recv()
+                out_ref[lines, c * width : (c + 1) * width] = (
+                    own[half_block, c] + part[lines] + recv_b[half_block, c].astype(jnp.float32)
+                ).astype(jnp.bfloat16)
 
     def pair(p):
         for c in range(chunks):
@@ -419,11 +451,20 @@
     project(0)
     work(2)
     pair(0)
+
+    @pl.when(frame == n - 1)
+    def _():
+        work(3)
+
     project(1)
     pair(1)
-    work(3)
+
+    @pl.when(jnp.logical_not(frame == n - 1))
+    def _():
+        work(3)
+
     project(2)
-    project(3)
+    conclude()
 
     wait_for(send_a.at[0:2], a_send)
     wait_for(send_b, b_send)
@@ -475,7 +516,7 @@
             dma((2,)),
             dma((2, pieces)),
             dma((2,)),
-            dma((pieces,)),
+            dma((pieces + 1,)),
             dma,
             dma((3, chunks)),
             dma,

time: 43.8 us -> 43.9 us (level)
  no operation moved by 1% of the time
where the time goes in v5:
time: 43.9 us; the launch traced here: 43.7 us
  Pallas kernels  43 us (98%)
  local copies, waits for them, and re-layouts  0.75 us (2%)
    pallas_call x1, Pallas kernels, fused(): pl.pallas_call(functools.partial(fused_kernel, n, chunks), out_shape=pltp...  43 us

profile of v5, /device:TPU:0, one launch (start us, length us, event | category | flops | bytes accessed | tf_op | source)
XLA Modules:
  0.0 43.7 jit_solution(12358246641993886990)
XLA Ops:
  0.0 43.0 %shard_map.64 = bf16[64,3072]{1,0:T(8,128)(2,1)S(1)} custom-call(bf16[4,2,32,768]{3,2,1,0:T(8,128)(2,1)} %bitcast.3, bf16[1,256,768]{2,1,0:T(8,128)(2,1)} %k_hbm.1, bf16[1,256,768]{2,1,0:T(8,128)(2,1)} %v_hbm.1, s32[4,4]{1,0:T(4,128)} %band_hbm.1, s32[7]{0:T(128)} %windows_hbm.1, bf16[768,3072]{1,0:T(8,128)(2,1)} %w_hbm.1), custom_call_target="tpu_custom_call" | custom-call | tf_op jit(solution)/shard_map/pallas_call | solution.py:496
  43.0 0.7 %copy.8 = bf16[1,64,3072]{2,1,0:T(8,128)(2,1)} copy(bf16[1,64,3072]{2,1,0:T(8,128)(2,1)S(1)} %bitcast.2) | data formatting | bytes 786432

commit v6 on v4

--- a/solution.py
+++ b/solution.py
@@ -132,7 +132,7 @@
         return pltpu.make_async_remote_copy(
             src_ref=source,
             dst_ref=target,
-            send_sem=in_send.at[h],
+            send_sem=in_send,
             recv_sem=landing(h, a),
             device_id={"tm": owner[h]},
             device_id_type=MESH,
@@ -427,11 +427,15 @@
 
     wait_for(send_a.at[0:2], a_send)
     wait_for(send_b, b_send)
-    for h in range(heads):
-
-        @pl.when(frame != owner[h])
-        def _():
-            wait_for(buf.at[0, 0, 0:3], in_send.at[h])
+    sent = 3 * length * HEAD // weight.shape[1]
+
+    @pl.when(both)
+    def _():
+        wait_for(weight.at[: (heads - 2) * sent], in_send)
+
+    @pl.when(jnp.logical_not(both))
+    def _():
+        wait_for(weight.at[: (heads - 1) * sent], in_send)
 
     wait_for(done.at[0, :, : n - 1], back_send.at[0])
 
@@ -471,7 +475,7 @@
             pltpu.VMEM((2, chunks, slab, part), jnp.bfloat16),
             pltpu.VMEM((2, chunks, slab, part), jnp.float32),
             pltpu.SemaphoreType.REGULAR((n,)),
-            dma((heads,)),
+            dma,
             dma((2,)),
             dma((2, pieces)),
             dma((2,)),
@@ -496,6 +500,7 @@
     def step(queries, keys, values, band_table, windows, out_weight):
         paired = mesh.shape["head"] == 2 and mesh.shape["sub"] == 2
         fits = queries.shape[0] == 1 and queries.shape[1] % 128 == 0
+        fits = fits and 3 * queries.shape[1] * HEAD % (8 * out_weight.shape[1]) == 0
         if n > 2 and paired and fits and queries.shape[2] == (2 * n - 2) * HEAD:
             return fused(n, queries, keys, values, band_table, windows, out_weight)
         return local(queries, keys, values, band_table, windows, out_weight)

time: 43.8 us -> 43.8 us (level)
  no operation moved by 1% of the time
where the time goes in v6:
time: 43.8 us; the launch traced here: 43.6 us
  Pallas kernels  42.9 us (98%)
  local copies, waits for them, and re-layouts  0.75 us (2%)
    pallas_call x1, Pallas kernels, fused(): pl.pallas_call(functools.partial(fused_kernel, n, chunks), out_shape=pltp...  42.9 us

profile of v6, /device:TPU:0, one launch (start us, length us, event | category | flops | bytes accessed | tf_op | source)
XLA Modules:
  0.0 43.6 jit_solution(12767087996484264100)
XLA Ops:
  0.0 42.9 %shard_map.64 = bf16[64,3072]{1,0:T(8,128)(2,1)S(1)} custom-call(bf16[4,2,32,768]{3,2,1,0:T(8,128)(2,1)} %bitcast.3, bf16[1,256,768]{2,1,0:T(8,128)(2,1)} %k_hbm.1, bf16[1,256,768]{2,1,0:T(8,128)(2,1)} %v_hbm.1, s32[4,4]{1,0:T(4,128)} %band_hbm.1, s32[7]{0:T(128)} %windows_hbm.1, bf16[768,3072]{1,0:T(8,128)(2,1)} %w_hbm.1), custom_call_target="tpu_custom_call" | custom-call | tf_op jit(solution)/shard_map/pallas_call | solution.py:459
  42.9 0.7 %copy.8 = bf16[1,64,3072]{2,1,0:T(8,128)(2,1)} copy(bf16[1,64,3072]{2,1,0:T(8,128)(2,1)S(1)} %bitcast.2) | data formatting | bytes 786432
